TPU v7x, 32 devices: a whole 2x2x4 slice. The times are simulated.
32 devices in a mesh: op: 8 (over y, x, core), sec: 4 (over z).
Axes of the slice: x: 2, y: 2, z: 4, core: 2. Of those that a mesh axis runs over, the one named last changes fastest.
Arguments:
- psi: bfloat16 [8, 512, 512], P('sec', 'op'), may hold values from -6 to 6
- left_ops: bfloat16 [16, 8, 512, 512], P('op', 'sec'), may hold values from -0.25 to 0.25
- right_ops: bfloat16 [16, 8, 512, 512], P('op', 'sec'), may hold values from -0.0625 to 0.0625
- conn: int32 [16, 8], P('op', 'sec'), may hold values from 0 to 7, as said below
- dims: int32 [8], P('sec'), may hold values from 128 to 512
Outputs:
- sigma: bfloat16 [8, 512, 512], P('sec', 'op')
Inputs may be any that keep to these rules, and one draw needn't show every extreme that they name: conn[k, s] lies in the same group of 2 consecutive sectors as s or in the next group, cyclically over the 8 sectors; both occur.
All inputs are finite; a program needn't handle non-finite values.
Results may differ from a plain program's by a relative error of at most 0.0049.
Values may be sent and summed in bfloat16 or wider, within the bound.
A program may use at most 64 MiB of HBM per device.

v0:
```python
import jax
import jax.numpy as jnp
from jax import lax
from jax.sharding import PartitionSpec as P


def from_behind(block, axis, distance):
    devices = range(lax.axis_size(axis))
    route = [((i - distance) % len(devices), i) for i in devices]
    return lax.ppermute(block, axis, route)


def row_mask(dims, row_start, rows, width):
    row_ids = row_start + jnp.arange(rows, dtype=jnp.int32)
    col_ids = jnp.arange(width, dtype=jnp.int32)
    return (row_ids[None, :, None] < dims[:, None, None]) & (
        col_ids[None, None, :] < dims[:, None, None]
    )


def on_device(psi, left_ops, right_ops, conn, dims):
    sdev, rows, width = psi.shape
    row_start = lax.axis_index("op") * rows
    masked = jnp.where(row_mask(dims, row_start, rows, width), psi, jnp.zeros_like(psi))
    gathered = lax.all_gather(masked, "op", axis=1, tiled=True)
    half = jnp.einsum(
        "ksij,sjm->ksim", left_ops, gathered, preferred_element_type=jnp.float32
    ).astype(jnp.bfloat16)
    term = jnp.einsum("ksim,ksnm->ksin", half, right_ops, preferred_element_type=jnp.float32)
    group = lax.axis_index("sec")
    slot = conn % sdev
    elsewhere = conn // sdev != group
    slots = jnp.arange(sdev, dtype=jnp.int32)
    hits = slot[:, :, None] == slots[None, None, :]
    own_hot = (hits & ~elsewhere[:, :, None]).astype(jnp.float32)
    next_hot = (hits & elsewhere[:, :, None]).astype(jnp.float32)
    own = jnp.einsum("kst,ksin->tin", own_hot, term, precision=lax.Precision.HIGHEST)
    onward = jnp.einsum("kst,ksin->tin", next_hot, term, precision=lax.Precision.HIGHEST)
    own_rows, onward_rows = (
        lax.psum_scatter(own, "op", scatter_dimension=1, tiled=True),
        lax.psum_scatter(onward, "op", scatter_dimension=1, tiled=True),
    )
    summed = own_rows + from_behind(onward_rows, "sec", 1)
    summed = jnp.where(row_mask(dims, row_start, rows, width), summed, jnp.zeros_like(summed))
    return summed.astype(jnp.bfloat16)


def solution(mesh):
    return jax.shard_map(
        on_device,
        mesh=mesh,
        in_specs=(
            P("sec", "op", None),
            P("op", "sec", None, None),
            P("op", "sec", None, None),
            P("op", "sec"),
            P("sec"),
        ),
        out_specs=P("sec", "op", None),
        check_vma=False,
    )
```

profile of v0, /device:TPU:0, one launch (start us, length us, event | category | flops | bytes accessed | tf_op | source)
XLA Modules:
  0.0 168.8 jit_solution(7087920952244045132)
XLA Ops:
  6.5 0.0 copy-start
  6.5 0.0 all-gather.2.cloned.1.call-start
  6.5 0.9 iota_compare_fusion
  7.4 0.7 broadcast_compare_fusion
  8.2 1.8 %and_select_fusion.1 = bf16[2,64,512]{2,0,1:T(2,128)(2,1)} fusion(pred[2,512]{1,0:T(4,128)(4,1)S(1)} %iota_compare_fusion, pred[2,64]{0,1:T(8,128)(4,1)S(1)} %broadcast_compare_fusion, bf16[2,64,512]{2,1,0:T(8,128)(2,1)} %param.5), kind=kLoop, calls=%fused_computation.12 | loop fusion | flops 131072 | bytes 263296 | tf_op jit(solution)/shard_map/jit(_where)/select_n | solution.py:24
  10.0 0.0 all-gather.2.cloned.1.call-update
  10.0 0.0 all-reduce.5.cloned.1.call-start
  10.0 0.7 and_select_fusion.3
  10.7 0.7 fusion.27
  11.4 24.8 %all-gather.2.cloned.1.call-done = bf16[2,512,512]{2,0,1:T(2,128)(2,1)} async-done(((bf16[2,64,512]{2,0,1:T(2,128)(2,1)}), bf16[2,512,512]{2,0,1:T(2,128)(2,1)}) %all-gather.2.cloned.1.call-update) | async-done | bytes 1048592 | tf_op jit(solution)/shard_map/all_gather | solution.py:25
  36.2 0.0 copy-done
  36.2 6.2 %fusion.4 = f32[2,2,512,512]{3,2,1,0:T(8,128)} fusion(bf16[2,2,512,512]{3,2,1,0:T(8,128)(2,1)S(1)} %copy-done, bf16[2,2,512,512]{3,2,1,0:T(8,128)(2,1)} %param.6, bf16[2,512,512,1]{2,0,1,3:T(2,128)(2,1)} %bitcast.19), kind=kOutput, calls=%fused_computation.4 | convolution fusion | flops 2148532224 | bytes 9437184 | tf_op jit(solution)/shard_map/ksim,ksnm->ksin/dot_general | solution.py:29
  42.5 0.0 copy-start.2
  42.5 15.5 %fusion.9 = f32[2,512,512]{2,0,1:T(2,128)} fusion(f32[2,2,512,512]{3,2,1,0:T(8,128)} %fusion.4, pred[2,2]{1,0:T(4,128)(4,1)S(1)} %get-tuple-element.7, s32[2,2]{1,0:T(2,128)S(1)} %and_select_fusion.3), kind=kOutput, calls=%fused_computation.8 | convolution fusion | flops 25165840 | bytes 6291476 | tf_op jit(solution)/shard_map/kst,ksin->tin/dot_general | solution.py:37
  58.0 0.0 copy-done.2
  58.0 10.5 %fusion.12 = f32[2,512,512]{2,0,1:T(2,128)} fusion(f32[2,2,512,512]{3,2,1,0:T(8,128)S(1)} %copy-done.2, pred[2,2]{1,0:T(4,128)(4,1)S(1)} %get-tuple-element.8, s32[2,2]{1,0:T(2,128)S(1)} %and_select_fusion.3), kind=kOutput, calls=%fused_computation.9 | convolution fusion | flops 25165840 | bytes 6291476 | tf_op jit(solution)/shard_map/kst,ksin->tin/dot_general | solution.py:38
  68.5 0.0 copy-start.1
  68.5 0.0 all-reduce.5.cloned.1.call-update
  68.5 0.6 copy-done.1
  69.1 0.6 dynamic-slice
  70.4 79.1 %all-reduce.5.cloned.1.call-done = (f32[2,512,512]{2,0,1:T(2,128)}, f32[2,512,512]{2,0,1:T(2,128)}) async-done(((f32[2,512,512]{2,0,1:T(2,128)}, f32[2,512,512]{2,0,1:T(2,128)}), (f32[2,512,512]{2,0,1:T(2,128)}, f32[2,512,512]{2,0,1:T(2,128)})) %all-reduce.5.cloned.1.call-update) | async-done | bytes 4194320
  149.5 1.0 constant_dynamic-slice_fusion
  150.4 1.5 collective-permute-start
  152.0 8.1 %collective-permute-done = f32[2,64,512]{2,0,1:T(2,128)S(1)} collective-permute-done((f32[2,64,512]{2,0,1:T(2,128)S(1)}, f32[2,64,512]{2,0,1:T(2,128)S(1)}, u32[]{:S(2)}, u32[]{:S(2)}) %collective-permute-start) | collective-permute-done | bytes 262176 | tf_op jit(solution)/shard_map/ppermute | solution.py:10
  160.1 1.2 fusion.17
  161.3 0.7 copy.13
  (1 shorter events, 0.0 us)
Async XLA Ops:
  6.5 29.7 %copy-start = (bf16[2,2,512,512]{3,2,1,0:T(8,128)(2,1)S(1)}, bf16[2,2,512,512]{3,2,1,0:T(8,128)(2,1)}, u32[]{:S(2)}) copy-start(bf16[2,2,512,512]{3,2,1,0:T(8,128)(2,1)} %param.7) | copy-start | bytes 6291460
  6.5 29.7 %all-gather.2.cloned.1.call-start = ((), (), s32[]{:S(2)}) async-start(), calls=%async_computation | async-start | bytes 1179648 | tf_op jit(solution)/shard_map/all_gather | solution.py:25
  10.0 139.5 %all-reduce.5.cloned.1.call-start = ((), (), s32[]{:S(2)}) async-start(), calls=%async_computation.1 | async-start | bytes 8388608
  42.5 15.5 %copy-start.2 = (f32[2,2,512,512]{3,2,1,0:T(8,128)S(1)}, f32[2,2,512,512]{3,2,1,0:T(8,128)}, u32[]{:S(2)}) copy-start(f32[2,2,512,512]{3,2,1,0:T(8,128)} %fusion.4) | copy-start | bytes 12582916
  68.5 0.7 copy-start.1
  150.4 9.7 %collective-permute-start = (f32[2,64,512]{2,0,1:T(2,128)S(1)}, f32[2,64,512]{2,0,1:T(2,128)S(1)}, u32[]{:S(2)}, u32[]{:S(2)}) collective-permute-start(f32[2,64,512]{2,0,1:T(2,128)S(1)} %constant_dynamic-slice_fusion), channel_id=1, source_target_pairs={{3,0},{0,1},{1,2},{2,3},{7,4},{4,5},{5,6},{6,7},{11,8},{8,9},{9,10... | collective-permute-start | bytes 786440 | tf_op jit(solution)/shard_map/ppermute | solution.py:10
Sparse Core Ops, SparseCore 0:
  10.1 26.0 all-gather.1
  68.6 80.8 all-reduce.4
where the time goes:
time: 169 us
  waiting for transfers between devices  112 us (66%)
  matrix products  32.2 us (19%)
  between operations  14.1 us (8%)
  other arithmetic  5.99 us (4%)
  local copies, waits for them, and re-layouts  2.85 us (2%)
    unnamed x3, waiting for transfers between devices  79.2 us
    all_gather x1, waiting for transfers between devices, on_device(): gathered = lax.all_gather(masked, 'op', axis=1, tiled=True)  24.8 us
    dot_general x1, matrix products, on_device(): jnp.einsum('kst,ksin->tin', own_hot, term, precision=lax.Precision.HIGHEST)  15.5 us
    dot_general x1, matrix products, on_device(): jnp.einsum('kst,ksin->tin', next_hot, term, precision=lax.Precision.HIGHEST)  10.5 us
    ppermute x1, waiting for transfers between devices, from_behind(): return lax.ppermute(block, axis, route)  8.13 us
    dot_general x1, matrix products, on_device(): jnp.einsum('ksim,ksnm->ksin', half, right_ops, preferred_element_type=jnp...  6.21 us
  transfers between devices with their start and end apart: 3, of which 3 were waited for; matrix products, arithmetic and copies ran while one was open for 1% of the time, Pallas kernels for 0%

commit v1 on v0

v1 whole, which is shorter than its diff:
```python
import functools

import jax
import jax.numpy as jnp
from jax import lax
from jax.experimental import pallas as pl
from jax.experimental.pallas import tpu as pltpu
from jax.sharding import PartitionSpec as P

MESH = pl.DeviceIdType.MESH


def flip(index, mask, size):
    out, bit = 0, 1
    while bit < size:
        out = out + ((index // bit + mask // bit) % 2) * bit
        bit *= 2
    return out


def kernel(
    n_op, n_sec,
    conn_ref, dims_ref, psi_ref, left_ref, right_ref, out_ref,
    left_v, right_v, got, masked, keep, give, from_core, sums, from_chip, onward, behind,
    load_sem, own_sem, ag_send, ag_recv, fwd_send, fwd_recv,
    core_send, core_recv, chip_send, chip_recv, z_send, z_recv,
):
    kdev, sdev, width, _ = left_ref.shape
    rows = psi_ref.shape[1]
    chips = n_op // 2
    me, sec = lax.axis_index("op"), lax.axis_index("sec")
    core, chip = me % 2, me // 2
    partner = chip * 2 + 1 - core
    after, before = (sec + 1) % n_sec, (sec + n_sec - 1) % n_sec

    def peer_of(j):
        return flip(chip, j, chips) * 2 + core

    loads = [pltpu.make_async_copy(psi_ref, got.at[me], own_sem.at[0])]
    loads[0].start()
    load_l = pltpu.make_async_copy(left_ref, left_v, load_sem.at[0])
    load_r = pltpu.make_async_copy(right_ref, right_v, load_sem.at[1])
    load_l.start()
    load_r.start()

    barrier = pltpu.get_barrier_semaphore()
    friends = [{"op": peer_of(j)} for j in range(1, chips)] + [{"op": partner}, {"sec": after}, {"sec": before}]
    for friend in friends:
        pl.semaphore_signal(barrier, inc=1, device_id=friend, device_id_type=MESH)
    pl.semaphore_wait(barrier, len(friends))

    def remote(src, dst, send, recv, device):
        copy = pltpu.make_async_remote_copy(
            src_ref=src, dst_ref=dst, send_sem=send, recv_sem=recv, device_id=device, device_id_type=MESH
        )
        return copy

    started = []
    gathers = {}
    for j in reversed(range(1, chips)):
        gathers[j] = remote(psi_ref, got.at[me], ag_send.at[j], ag_recv.at[j], {"op": peer_of(j)})
        gathers[j].start()
    shares = {0: remote(psi_ref, got.at[me], fwd_send.at[0], fwd_recv.at[0], {"op": partner})}
    shares[0].start()
    for j in range(1, chips):
        gathers[j].wait_recv()
        peer = peer_of(j)
        shares[j] = remote(got.at[peer], got.at[peer], fwd_send.at[j], fwd_recv.at[j], {"op": partner})
        shares[j].start()
    loads[0].wait()
    for j in range(chips):
        shares[j].wait_recv()
    for d in range(n_op):
        row = d * rows + lax.broadcasted_iota(jnp.int32, (rows, width), 0)
        col = lax.broadcasted_iota(jnp.int32, (rows, width), 1)
        for s in range(sdev):
            inside = (row < dims_ref[s]) & (col < dims_ref[s])
            masked[s, d * rows:(d + 1) * rows, :] = jnp.where(inside, got[d, s], jnp.zeros((), got.dtype))
    load_l.wait()
    load_r.wait()

    weights = {}
    for k in range(kdev):
        for s in range(sdev):
            away = (conn_ref[k, s] // sdev != sec).astype(jnp.int32)
            slot = conn_ref[k, s] % sdev
            for g in range(2):
                for t in range(sdev):
                    hit = ((slot == t) & (away == 1 - g)).astype(jnp.float32)
                    weights[k, s, g, t] = hit

    core_copies, chip_copies = {}, {}

    def compute(j):
        first = pl.multiple_of(flip(chip, j, chips) * (2 * rows), 2 * rows)
        terms = {}
        for s in range(sdev):
            lhs = left_v[:, s, pl.ds(first, 2 * rows), :].reshape(kdev * 2 * rows, width)
            half = jnp.dot(lhs, masked[s], preferred_element_type=jnp.float32).astype(jnp.bfloat16)
            for k in range(kdev):
                terms[k, s] = lax.dot_general(
                    half[k * 2 * rows:(k + 1) * 2 * rows], right_v[k, s],
                    (((1,), (1,)), ((), ())), preferred_element_type=jnp.float32,
                )
        for g in range(2):
            for t in range(sdev):
                total = sum(weights[k, s, g, t] * terms[k, s] for k in range(kdev) for s in range(sdev))
                keep[j, g, t] = total
                give[j, g, t] = total.astype(jnp.bfloat16)
        theirs = pl.multiple_of((1 - core) * rows, rows)
        for g in range(2):
            core_copies[j, g] = remote(
                give.at[j, g, :, pl.ds(theirs, rows), :], from_core.at[j, g],
                core_send.at[j, g], core_recv.at[j, g], {"op": partner},
            )
            core_copies[j, g].start()

    def pair_sum(j, g):
        core_copies[j, g].wait_recv()
        mine = pl.multiple_of(core * rows, rows)
        return keep[j, g, :, pl.ds(mine, rows), :] + from_core[j, g].astype(jnp.float32)

    def pass_on(j):
        for g in range(2):
            sums[j, g] = pair_sum(j, g).astype(jnp.bfloat16)
            chip_copies[j, g] = remote(
                sums.at[j, g], from_chip.at[j, g], chip_send.at[j, g], chip_recv.at[j, g], {"op": peer_of(j)}
            )
            chip_copies[j, g].start()

    for j in reversed(range(chips)):
        compute(j)
        if j + 1 < chips:
            pass_on(j + 1)

    def collect(g):
        total = pair_sum(0, g)
        for j in reversed(range(1, chips)):
            chip_copies[j, g].wait_recv()
            total = total + from_chip[j, g].astype(jnp.float32)
        return total

    onward[...] = collect(0).astype(jnp.bfloat16)
    shift = remote(onward, behind, z_send.at[0], z_recv.at[0], {"sec": after})
    shift.start()
    own = collect(1)
    keep[0, 1, :, 0:rows, :] = own
    shift.wait_recv()
    for s in range(sdev):
        row = me * rows + lax.broadcasted_iota(jnp.int32, (rows, width), 0)
        col = lax.broadcasted_iota(jnp.int32, (rows, width), 1)
        inside = (row < dims_ref[s]) & (col < dims_ref[s])
        value = keep[0, 1, s, 0:rows, :] + behind[s].astype(jnp.float32)
        out_ref[s] = jnp.where(inside, value, jnp.zeros_like(value)).astype(out_ref.dtype)

    for copies in (gathers, shares, core_copies, chip_copies, {0: shift}):
        for copy in copies.values():
            copy.wait_send()


def on_device(n_op, n_sec, psi, left_ops, right_ops, conn, dims):
    sdev, rows, width = psi.shape
    kdev = left_ops.shape[0]
    chips = n_op // 2
    bf16, f32 = jnp.bfloat16, jnp.float32
    dma = pltpu.SemaphoreType.DMA
    smem = pl.BlockSpec(memory_space=pltpu.SMEM)
    hbm = pl.BlockSpec(memory_space=pl.ANY)
    return pl.pallas_call(
        functools.partial(kernel, n_op, n_sec),
        out_shape=jax.ShapeDtypeStruct(psi.shape, psi.dtype),
        in_specs=[smem, smem, hbm, hbm, hbm],
        out_specs=pl.BlockSpec(memory_space=pltpu.VMEM),
        scratch_shapes=[
            pltpu.VMEM(left_ops.shape, bf16),
            pltpu.VMEM(right_ops.shape, bf16),
            pltpu.VMEM((n_op, sdev, rows, width), bf16),
            pltpu.VMEM((sdev, width, width), bf16),
            pltpu.VMEM((chips, 2, sdev, 2 * rows, width), f32),
            pltpu.VMEM((chips, 2, sdev, 2 * rows, width), bf16),
            pltpu.VMEM((chips, 2, sdev, rows, width), bf16),
            pltpu.VMEM((chips, 2, sdev, rows, width), bf16),
            pltpu.VMEM((chips, 2, sdev, rows, width), bf16),
            pltpu.VMEM((sdev, rows, width), bf16),
            pltpu.VMEM((sdev, rows, width), bf16),
            dma((2,)),
            dma((1,)),
            dma((chips,)), dma((chips,)),
            dma((chips,)), dma((chips,)),
            dma((chips, 2)), dma((chips, 2)),
            dma((chips, 2)), dma((chips, 2)),
            dma((1,)), dma((1,)),
        ],
        compiler_params=pltpu.CompilerParams(
            collective_id=0, has_side_effects=True, vmem_limit_bytes=48 * 1024 * 1024
        ),
    )(conn, dims, psi, left_ops, right_ops)


def solution(mesh):
    return jax.shard_map(
        functools.partial(on_device, mesh.shape["op"], mesh.shape["sec"]),
        mesh=mesh,
        in_specs=(
            P("sec", "op", None),
            P("op", "sec", None, None),
            P("op", "sec", None, None),
            P("op", "sec"),
            P("sec"),
        ),
        out_specs=P("sec", "op", None),
        check_vma=False,
    )
```

time: 169 us -> 41.4 us (0.24)
  waiting for transfers between devices: 112 us -> 0 us
  Pallas kernels: 0 us -> 35.1 us
  matrix products: 32.2 us -> 0 us
  between operations: 14.1 us -> 0.01 us
  other arithmetic: 5.99 us -> 0 us
  local copies, waits for them, and re-layouts: 2.85 us -> 6.08 us
    unnamed x3 -> x0, waiting for transfers between devices: 79.2 us -> none
    pallas_call x0 -> x1, Pallas kernels: none -> 35.1 us  [on_device(): pl.pallas_call(functools.partial(kernel, n_op, n_sec), out_shape=jax.Shap...]
    dot_general x3 -> x0, matrix products: 32.2 us -> none  [the longest x1 15.5 us: on_device(): jnp.einsum('kst,ksin->tin', own_hot, term, precision=lax.Precision.HIGHEST)]
    all_gather x1 -> x0, waiting for transfers between devices: 24.8 us -> none  [on_device(): gathered = lax.all_gather(masked, 'op', axis=1, tiled=True)]
    ppermute x1 -> x0, waiting for transfers between devices: 8.13 us -> none  [from_behind(): return lax.ppermute(block, axis, route)]
    unnamed x8 -> x11, local copies, waits for them, and re-layouts: 2.18 us -> 6.08 us
    select_n x2 -> x0, other arithmetic: 2.5 us -> none  [the longest x1 1.81 us: on_device(): jnp.where(row_mask(dims, row_start, rows, width), psi, jnp.zeros_like(psi))]
  transfers between devices with their start and end apart: 3 -> 0, of which waited for: 3 -> 0; matrix products, arithmetic and copies ran while one was open for 1% -> 0% of each run, Pallas kernels for 0% -> 0%
where the time goes in v1:
time: 41.4 us; the launch traced here: 41.2 us
  Pallas kernels  35.1 us (85%)
  local copies, waits for them, and re-layouts  6.08 us (15%)
    pallas_call x1, Pallas kernels, on_device(): pl.pallas_call(functools.partial(kernel, n_op, n_sec), out_shape=jax.Shap...  35.1 us
    unnamed x11, local copies, waits for them, and re-layouts  6.08 us

profile of v1, /device:TPU:0, one launch (start us, length us, event | category | flops | bytes accessed | tf_op | source)
XLA Modules:
  0.0 41.2 jit_solution(15855967758294878760)
XLA Ops:
  0.0 0.0 copy-start
  0.0 1.6 %copy-done = bf16[2,2,512,512]{3,2,1,0:T(8,128)(2,1)S(1)} copy-done((bf16[2,2,512,512]{3,2,1,0:T(8,128)(2,1)S(1)}, bf16[2,2,512,512]{3,2,1,0:T(8,128)(2,1)}, u32[]{:S(2)}) %copy-start) | copy-done | bytes 2097176
  1.6 0.0 copy-start.1
  1.6 1.6 %copy-done.1 = bf16[2,2,512,512]{3,2,1,0:T(8,128)(2,1)S(1)} copy-done((bf16[2,2,512,512]{3,2,1,0:T(8,128)(2,1)S(1)}, bf16[2,2,512,512]{3,2,1,0:T(8,128)(2,1)}, u32[]{:S(2)}) %copy-start.1) | copy-done | bytes 2097176
  3.2 0.0 copy-start.2
  3.2 0.9 %copy-done.2 = bf16[2,64,512]{2,1,0:T(8,128)(2,1)S(1)} copy-done((bf16[2,64,512]{2,1,0:T(8,128)(2,1)S(1)}, bf16[2,64,512]{2,1,0:T(8,128)(2,1)}, u32[]{:S(2)}) %copy-start.2) | copy-done | bytes 131096
  4.1 0.0 copy-start.3
  4.1 0.7 %copy-done.3 = s32[2,2]{1,0:T(2,128)S(1)} copy-done((s32[2,2]{1,0:T(2,128)S(1)}, s32[2,2]{1,0:T(2,128)}, u32[]{:S(2)}) %copy-start.3) | copy-done | bytes 40
  4.8 0.0 copy-start.4
  4.8 0.7 %copy-done.4 = s32[2]{0:T(128)S(1)} copy-done((s32[2]{0:T(128)S(1)}, s32[2]{0:T(128)}, u32[]{:S(2)}) %copy-start.4) | copy-done | bytes 32
  5.4 35.1 %shard_map.55 = bf16[2,64,512]{2,1,0:T(8,128)(2,1)S(1)} custom-call(s32[2,2]{1,0:T(2,128)S(1)} %copy-done.3, s32[2]{0:T(128)S(1)} %copy-done.4, bf16[2,64,512]{2,1,0:T(8,128)(2,1)S(1)} %copy-done.2, bf16[2,2,512,512]{3,2,1,0:T(8,128)(2,1)S(1)} %copy-done, bf16[2,2,512,512]{3,2,1,0:T(8,128)(2,1)S(1)} %copy-done.1), custom_call_target="tpu_custom_call" | custom-call | tf_op jit(solution)/shard_map/pallas_call | solution.py:169
  40.6 0.7 %copy.7 = bf16[2,64,512]{2,1,0:T(8,128)(2,1)} copy(bf16[2,64,512]{2,1,0:T(8,128)(2,1)S(1)} %shard_map.55) | data formatting | bytes 262144
Async XLA Ops:
  0.0 1.6 %copy-start = (bf16[2,2,512,512]{3,2,1,0:T(8,128)(2,1)S(1)}, bf16[2,2,512,512]{3,2,1,0:T(8,128)(2,1)}, u32[]{:S(2)}) copy-start(bf16[2,2,512,512]{3,2,1,0:T(8,128)(2,1)} %left_ref.1) | copy-start | bytes 6291460
  1.6 1.6 %copy-start.1 = (bf16[2,2,512,512]{3,2,1,0:T(8,128)(2,1)S(1)}, bf16[2,2,512,512]{3,2,1,0:T(8,128)(2,1)}, u32[]{:S(2)}) copy-start(bf16[2,2,512,512]{3,2,1,0:T(8,128)(2,1)} %right_ref.1) | copy-start | bytes 6291460
  3.2 0.9 %copy-start.2 = (bf16[2,64,512]{2,1,0:T(8,128)(2,1)S(1)}, bf16[2,64,512]{2,1,0:T(8,128)(2,1)}, u32[]{:S(2)}) copy-start(bf16[2,64,512]{2,1,0:T(8,128)(2,1)} %psi_ref.1) | copy-start | bytes 393220
  4.1 0.7 %copy-start.3 = (s32[2,2]{1,0:T(2,128)S(1)}, s32[2,2]{1,0:T(2,128)}, u32[]{:S(2)}) copy-start(s32[2,2]{1,0:T(2,128)} %conn_ref.1) | copy-start | bytes 52
  4.8 0.7 %copy-start.4 = (s32[2]{0:T(128)S(1)}, s32[2]{0:T(128)}, u32[]{:S(2)}) copy-start(s32[2]{0:T(128)} %dims_ref.1) | copy-start | bytes 28

commit v2 on v1

v2 whole, which is shorter than its diff:
```python
import functools

import jax
import jax.numpy as jnp
from jax import lax
from jax.experimental import pallas as pl
from jax.experimental.pallas import tpu as pltpu
from jax.sharding import PartitionSpec as P

MESH = pl.DeviceIdType.MESH


def flip(index, mask, size):
    out, bit = 0, 1
    while bit < size:
        out = out + ((index // bit + mask // bit) % 2) * bit
        bit *= 2
    return out


def kernel(
    n_op, n_sec,
    conn_hbm, dims_hbm, psi_ref, left_ref, right_ref, out_ref,
    conn_ref, dims_ref,
    left_v, right_v, got, masked, keep, give, from_core, early, arrived, sums, from_chip, onward, behind,
    load_sem, own_sem, ag_send, ag_recv, fwd_send, fwd_recv,
    core_send, core_recv, ahead_send, ahead_recv, chip_send, chip_recv, z_send, z_recv,
):
    kdev, sdev, width, _ = left_ref.shape
    rows = psi_ref.shape[1]
    chips = n_op // 2
    me, sec = lax.axis_index("op"), lax.axis_index("sec")
    core, chip = me % 2, me // 2
    partner = chip * 2 + 1 - core
    after, before = (sec + 1) % n_sec, (sec + n_sec - 1) % n_sec

    def peer_of(j):
        return flip(chip, j, chips) * 2 + core

    loads = [pltpu.make_async_copy(psi_ref, got.at[me], own_sem.at[0])]
    loads[0].start()
    load_l = pltpu.make_async_copy(left_ref, left_v, load_sem.at[0])
    load_r = pltpu.make_async_copy(right_ref, right_v, load_sem.at[1])
    load_conn = pltpu.make_async_copy(conn_hbm, conn_ref, load_sem.at[2])
    load_dims = pltpu.make_async_copy(dims_hbm, dims_ref, load_sem.at[3])
    load_conn.start()
    load_dims.start()
    load_l.start()
    load_r.start()

    barrier = pltpu.get_barrier_semaphore()
    friends = [{"op": peer_of(j)} for j in range(1, chips)] + [{"op": partner}, {"sec": after}, {"sec": before}]
    for friend in friends:
        pl.semaphore_signal(barrier, inc=1, device_id=friend, device_id_type=MESH)
    pl.semaphore_wait(barrier, len(friends))

    def remote(src, dst, send, recv, device):
        copy = pltpu.make_async_remote_copy(
            src_ref=src, dst_ref=dst, send_sem=send, recv_sem=recv, device_id=device, device_id_type=MESH
        )
        return copy

    half_s, half_r = sdev // 2, rows // 2
    relayed = chips == 4
    order = [1, 2, 3] if relayed else list(range(1, chips))
    sent = []

    def go(copy):
        copy.start()
        sent.append(copy)
        return copy

    def part(r):
        return pl.ds(r * half_s, half_s)

    gathers, shares = {}, {}
    for first in (0, 1):
        for j in order[:2] if relayed else order:
            r = first if j % 2 == 1 else 1 - first
            gathers[j, r] = go(remote(
                psi_ref.at[part(r)], got.at[me, part(r)], ag_send.at[j, r], ag_recv.at[j, r], {"op": peer_of(j)}
            ))
    for r in (0, 1):
        shares[0, r] = go(remote(
            psi_ref.at[part(r)], got.at[me, part(r)], fwd_send.at[0, r], fwd_recv.at[0, r], {"op": partner}
        ))
    if relayed:
        arrivals = [(1, 0), (2, 1), (1, 1), (2, 0), (3, 0), (3, 1)]
    else:
        arrivals = [(j, r) for j in order for r in (0, 1)]

    def forward(j, r):
        gathers[j, r].wait_recv()
        slab = got.at[peer_of(j), part(r)]
        if relayed and (j, r) in ((1, 0), (2, 1)):
            gathers[3, r] = go(remote(slab, slab, ag_send.at[3, r], ag_recv.at[3, r], {"op": peer_of(3 - j)}))
        shares[j, r] = go(remote(slab, slab, fwd_send.at[j, r], fwd_recv.at[j, r], {"op": partner}))

    def mask_in(d):
        row = d * rows + lax.broadcasted_iota(jnp.int32, (rows, width), 0)
        col = lax.broadcasted_iota(jnp.int32, (rows, width), 1)
        for s in range(sdev):
            inside = (row < dims_ref[s]) & (col < dims_ref[s])
            masked[s, pl.ds(pl.multiple_of(d * rows, rows), rows), :] = jnp.where(
                inside, got[d, s], jnp.zeros((), got.dtype)
            )

    def mask_shared(j):
        for r in (0, 1):
            shares[j, r].wait_recv()
        mask_in(flip(chip, j, chips) * 2 + 1 - core)

    for j, r in arrivals[:4]:
        forward(j, r)
    loads[0].wait()
    load_conn.wait()
    load_dims.wait()
    mask_in(me)
    for j in order[:2]:
        mask_in(peer_of(j))
    for j in [0] + order[:2]:
        mask_shared(j)
    for j, r in arrivals[4:]:
        forward(j, r)
    for j in order[2:]:
        mask_in(peer_of(j))
    for j in order[2:]:
        mask_shared(j)
    load_l.wait()
    load_r.wait()

    weights = {}
    for k in range(kdev):
        for s in range(sdev):
            away = (conn_ref[k, s] // sdev != sec).astype(jnp.int32)
            slot = conn_ref[k, s] % sdev
            for g in range(2):
                for t in range(sdev):
                    hit = ((slot == t) & (away == 1 - g)).astype(jnp.float32)
                    weights[k, s, g, t] = hit

    core_copies = {}

    def compute(j):
        first = pl.multiple_of(flip(chip, j, chips) * (2 * rows), 2 * rows)
        terms = {}
        for s in range(sdev):
            lhs = left_v[:, s, pl.ds(first, 2 * rows), :].reshape(kdev * 2 * rows, width)
            half = jnp.dot(lhs, masked[s], preferred_element_type=jnp.float32).astype(jnp.bfloat16)
            for k in range(kdev):
                terms[k, s] = lax.dot_general(
                    half[k * 2 * rows:(k + 1) * 2 * rows], right_v[k, s],
                    (((1,), (1,)), ((), ())), preferred_element_type=jnp.float32,
                )
        theirs = pl.multiple_of((1 - core) * rows, rows)
        for g in range(2):
            for t in range(sdev):
                total = sum(weights[k, s, g, t] * terms[k, s] for k in range(kdev) for s in range(sdev))
                keep[j, g, t] = total
                give[j, g, t] = total.astype(jnp.bfloat16)
        for g in range(2):
            core_copies[j, g] = go(remote(
                give.at[j, g, :, pl.ds(theirs, rows), :], from_core.at[j, g],
                core_send.at[j, g], core_recv.at[j, g], {"op": partner},
            ))

    group_of, slots_of = (0, 1, 1), (1, 1, 0)

    def pair_sum(j, g, r_slot, r=None):
        start, count = (0, rows) if r is None else (r * half_r, half_r)
        mine = pl.multiple_of(core * rows + start, half_r)
        slots = slice(r_slot * half_s, (r_slot + 1) * half_s)
        return keep[j, g, slots, pl.ds(mine, count), :] + from_core[
            j, g, slots, start:start + count, :
        ].astype(jnp.float32)

    ahead, chip_copies = {}, {}

    def send_ahead(j):
        core_copies[j, 0].wait_recv()
        early[j] = pair_sum(j, 0, 0).astype(jnp.bfloat16)
        ahead[j] = go(remote(early.at[j], arrived.at[j], ahead_send.at[j], ahead_recv.at[j], {"sec": after}))

    def is_relay(j):
        return relayed and j == 3

    def needs_relay(j, r):
        return relayed and (j, r) in ((1, 1), (2, 0))

    def send_piece(j, p, r):
        value = pair_sum(j, group_of[p], slots_of[p], r)
        rs = slice(r * half_r, (r + 1) * half_r)
        if p == 2:
            value = value + arrived[j, :, rs, :].astype(jnp.float32)
        if needs_relay(j, r):
            chip_copies[3, p, r].wait_recv()
            value = value + from_chip[3, p, :, rs, :].astype(jnp.float32)
        sums[j, p, :, rs, :] = value.astype(jnp.bfloat16)
        via = (1 if r == 0 else 2) if is_relay(j) else j
        chip_copies[j, p, r] = go(remote(
            sums.at[j, p, :, rs, :], from_chip.at[j, p, :, rs, :],
            chip_send.at[j, p, r], chip_recv.at[j, p, r], {"op": peer_of(via)},
        ))

    def send_now(j, p):
        for r in (0, 1):
            if not needs_relay(j, r):
                send_piece(j, p, r)

    def handle(j):
        send_ahead(j)
        send_now(j, 0)
        core_copies[j, 1].wait_recv()
        send_now(j, 1)

    chunks = list(reversed(order)) + [0]
    for i, j in enumerate(chunks):
        compute(j)
        if i >= 1:
            handle(chunks[i - 1])
    if order:
        ahead[order[-1]].wait_recv()
        send_now(order[-1], 2)
    if relayed:
        for p in (0, 1):
            send_piece(1, p, 1)
            send_piece(2, p, 0)
    send_ahead(0)
    core_copies[0, 1].wait_recv()
    for j in reversed(order[:-1]):
        ahead[j].wait_recv()
        send_now(j, 2)
    if relayed:
        send_piece(1, 2, 1)
        send_piece(2, 2, 0)

    sources = order[:2] if relayed else order

    def collect(p):
        total = pair_sum(0, group_of[p], slots_of[p])
        for j in sources:
            for r in (0, 1):
                chip_copies[j, p, r].wait_recv()
            total = total + from_chip[j, p].astype(jnp.float32)
        return total

    onward[...] = collect(0).astype(jnp.bfloat16)
    shift = go(remote(onward, behind, z_send.at[0], z_recv.at[0], {"sec": after}))

    def put(slot, value):
        row = me * rows + lax.broadcasted_iota(jnp.int32, (rows, width), 0)
        col = lax.broadcasted_iota(jnp.int32, (rows, width), 1)
        for i in range(half_s):
            s = slot * half_s + i
            inside = (row < dims_ref[s]) & (col < dims_ref[s])
            out_ref[s] = jnp.where(inside, value[i], jnp.zeros_like(value[i])).astype(out_ref.dtype)

    own = collect(1)
    ahead[0].wait_recv()
    put(0, collect(2) + arrived[0].astype(jnp.float32))
    shift.wait_recv()
    put(1, own + behind[...].astype(jnp.float32))

    for copy in sent:
        copy.wait_send()


def on_device(n_op, n_sec, psi, left_ops, right_ops, conn, dims):
    sdev, rows, width = psi.shape
    kdev = left_ops.shape[0]
    chips, half = n_op // 2, sdev // 2
    bf16, f32 = jnp.bfloat16, jnp.float32
    dma = pltpu.SemaphoreType.DMA
    hbm = pl.BlockSpec(memory_space=pl.ANY)
    return pl.pallas_call(
        functools.partial(kernel, n_op, n_sec),
        out_shape=jax.ShapeDtypeStruct(psi.shape, psi.dtype),
        in_specs=[hbm] * 5,
        out_specs=pl.BlockSpec(memory_space=pltpu.VMEM),
        scratch_shapes=[
            pltpu.SMEM(conn.shape, conn.dtype),
            pltpu.SMEM(dims.shape, dims.dtype),
            pltpu.VMEM(left_ops.shape, bf16),
            pltpu.VMEM(right_ops.shape, bf16),
            pltpu.VMEM((n_op, sdev, rows, width), bf16),
            pltpu.VMEM((sdev, width, width), bf16),
            pltpu.VMEM((chips, 2, sdev, 2 * rows, width), f32),
            pltpu.VMEM((chips, 2, sdev, 2 * rows, width), bf16),
            pltpu.VMEM((chips, 2, sdev, rows, width), bf16),
            pltpu.VMEM((chips, half, rows, width), bf16),
            pltpu.VMEM((chips, half, rows, width), bf16),
            pltpu.VMEM((chips, 3, half, rows, width), bf16),
            pltpu.VMEM((chips, 3, half, rows, width), bf16),
            pltpu.VMEM((half, rows, width), bf16),
            pltpu.VMEM((half, rows, width), bf16),
            dma((4,)),
            dma((1,)),
            dma((chips, 2)), dma((chips, 2)),
            dma((chips, 2)), dma((chips, 2)),
            dma((chips, 2)), dma((chips, 2)),
            dma((chips,)), dma((chips,)),
            dma((chips, 3, 2)), dma((chips, 3, 2)),
            dma((1,)), dma((1,)),
        ],
        compiler_params=pltpu.CompilerParams(
            collective_id=0, has_side_effects=True, vmem_limit_bytes=60 * 1024 * 1024
        ),
    )(conn, dims, psi, left_ops, right_ops)


def solution(mesh):
    return jax.shard_map(
        functools.partial(on_device, mesh.shape["op"], mesh.shape["sec"]),
        mesh=mesh,
        in_specs=(
            P("sec", "op", None),
            P("op", "sec", None, None),
            P("op", "sec", None, None),
            P("op", "sec"),
            P("sec"),
        ),
        out_specs=P("sec", "op", None),
        check_vma=False,
    )
```

time: 41.4 us -> 31.6 us (0.76)
  Pallas kernels: 35.1 us -> 29.9 us
  local copies, waits for them, and re-layouts: 6.08 us -> 1.57 us
    pallas_call x1, Pallas kernels: 35.1 us -> 29.9 us  [on_device(): pl.pallas_call(functools.partial(kernel, n_op, n_sec), out_shape=jax.Shap...]
    unnamed x11 -> x1, local copies, waits for them, and re-layouts: 6.08 us -> 1.57 us
where the time goes in v2:
time: 31.6 us; the launch traced here: 31.5 us
  Pallas kernels  29.9 us (95%)
  local copies, waits for them, and re-layouts  1.57 us (5%)
    pallas_call x1, Pallas kernels, on_device(): pl.pallas_call(functools.partial(kernel, n_op, n_sec), out_shape=jax.Shap...  29.9 us
    unnamed x1, local copies, waits for them, and re-layouts  1.57 us

profile of v2, /device:TPU:0, one launch (start us, length us, event | category | flops | bytes accessed | tf_op | source)
XLA Modules:
  0.0 31.5 jit_solution(4349058074374135912)
XLA Ops:
  0.0 29.9 %shard_map.55 = bf16[2,64,512]{2,1,0:T(8,128)(2,1)} custom-call(s32[2,2]{1,0:T(2,128)} %conn_hbm.1, s32[2]{0:T(128)} %dims_hbm.1, bf16[2,64,512]{2,1,0:T(8,128)(2,1)} %psi_ref.1, bf16[2,2,512,512]{3,2,1,0:T(8,128)(2,1)} %left_ref.1, bf16[2,2,512,512]{3,2,1,0:T(8,128)(2,1)} %right_ref.1), custom_call_target="tpu_custom_call" | custom-call | tf_op jit(solution)/shard_map/pallas_call | solution.py:275
  29.9 1.6 %copy.7 = bf16[2,64,512]{2,1,0:T(8,128)(2,1)} copy(bf16[2,64,512]{2,1,0:T(8,128)(2,1)} %shard_map.55) | data formatting | bytes 262144

commit v3 on v2

--- a/solution.py
+++ b/solution.py
@@ -22,7 +22,7 @@
     n_op, n_sec,
     conn_hbm, dims_hbm, psi_ref, left_ref, right_ref, out_ref,
     conn_ref, dims_ref,
-    left_v, right_v, got, masked, keep, give, from_core, early, arrived, sums, from_chip, onward, behind,
+    left_v, right_v, got, masked, begun, keep, give, from_core, early, arrived, sums, from_chip, onward, behind,
     load_sem, own_sem, ag_send, ag_recv, fwd_send, fwd_recv,
     core_send, core_recv, ahead_send, ahead_recv, chip_send, chip_recv, z_send, z_recv,
 ):
@@ -74,60 +74,57 @@
         return pl.ds(r * half_s, half_s)
 
     gathers, shares = {}, {}
-    for first in (0, 1):
-        for j in order[:2] if relayed else order:
-            r = first if j % 2 == 1 else 1 - first
-            gathers[j, r] = go(remote(
-                psi_ref.at[part(r)], got.at[me, part(r)], ag_send.at[j, r], ag_recv.at[j, r], {"op": peer_of(j)}
-            ))
     for r in (0, 1):
         shares[0, r] = go(remote(
             psi_ref.at[part(r)], got.at[me, part(r)], fwd_send.at[0, r], fwd_recv.at[0, r], {"op": partner}
         ))
-    if relayed:
-        arrivals = [(1, 0), (2, 1), (1, 1), (2, 0), (3, 0), (3, 1)]
-    else:
-        arrivals = [(j, r) for j in order for r in (0, 1)]
-
-    def forward(j, r):
-        gathers[j, r].wait_recv()
-        slab = got.at[peer_of(j), part(r)]
-        if relayed and (j, r) in ((1, 0), (2, 1)):
-            gathers[3, r] = go(remote(slab, slab, ag_send.at[3, r], ag_recv.at[3, r], {"op": peer_of(3 - j)}))
-        shares[j, r] = go(remote(slab, slab, fwd_send.at[j, r], fwd_recv.at[j, r], {"op": partner}))
-
-    def mask_in(d):
+    for r in (0, 1):
+        for j in reversed(order):
+            gathers[j, r] = go(remote(
+                psi_ref.at[part(r)], got.at[me, part(r)], ag_send.at[j, r], ag_recv.at[j, r], {"op": peer_of(j)}
+            ))
+
+    def mask_in(d, r):
         row = d * rows + lax.broadcasted_iota(jnp.int32, (rows, width), 0)
         col = lax.broadcasted_iota(jnp.int32, (rows, width), 1)
-        for s in range(sdev):
+        for s in range(r * half_s, (r + 1) * half_s):
             inside = (row < dims_ref[s]) & (col < dims_ref[s])
             masked[s, pl.ds(pl.multiple_of(d * rows, rows), rows), :] = jnp.where(
                 inside, got[d, s], jnp.zeros((), got.dtype)
             )
 
-    def mask_shared(j):
-        for r in (0, 1):
+    def gather(r):
+        for j in order:
+            gathers[j, r].wait_recv()
+            slab = got.at[peer_of(j), part(r)]
+            shares[j, r] = go(remote(slab, slab, fwd_send.at[j, r], fwd_recv.at[j, r], {"op": partner}))
+        for j in [0] + order:
+            mask_in(peer_of(j), r)
+        for j in [0] + order:
             shares[j, r].wait_recv()
-        mask_in(flip(chip, j, chips) * 2 + 1 - core)
-
-    for j, r in arrivals[:4]:
-        forward(j, r)
+            mask_in(flip(chip, j, chips) * 2 + 1 - core, r)
+
+    def terms_of(j, s):
+        first = pl.multiple_of(flip(chip, j, chips) * (2 * rows), 2 * rows)
+        lhs = left_v[:, s, pl.ds(first, 2 * rows), :].reshape(kdev * 2 * rows, width)
+        half = jnp.dot(lhs, masked[s], preferred_element_type=jnp.float32).astype(jnp.bfloat16)
+        return [lax.dot_general(
+            half[k * 2 * rows:(k + 1) * 2 * rows], right_v[k, s],
+            (((1,), (1,)), ((), ())), preferred_element_type=jnp.float32,
+        ) for k in range(kdev)]
+
+    chunks = list(reversed(order)) + [0]
     loads[0].wait()
     load_conn.wait()
     load_dims.wait()
-    mask_in(me)
-    for j in order[:2]:
-        mask_in(peer_of(j))
-    for j in [0] + order[:2]:
-        mask_shared(j)
-    for j, r in arrivals[4:]:
-        forward(j, r)
-    for j in order[2:]:
-        mask_in(peer_of(j))
-    for j in order[2:]:
-        mask_shared(j)
+    gather(0)
     load_l.wait()
     load_r.wait()
+    for j in chunks[:2]:
+        for s in range(half_s):
+            for k, value in enumerate(terms_of(j, s)):
+                begun[j, k, s] = value
+    gather(1)
 
     weights = {}
     for k in range(kdev):
@@ -142,29 +139,26 @@
     core_copies = {}
 
     def compute(j):
-        first = pl.multiple_of(flip(chip, j, chips) * (2 * rows), 2 * rows)
         terms = {}
         for s in range(sdev):
-            lhs = left_v[:, s, pl.ds(first, 2 * rows), :].reshape(kdev * 2 * rows, width)
-            half = jnp.dot(lhs, masked[s], preferred_element_type=jnp.float32).astype(jnp.bfloat16)
+            if s < half_s and j in chunks[:2]:
+                values = [begun[j, k, s] for k in range(kdev)]
+            else:
+                values = terms_of(j, s)
             for k in range(kdev):
-                terms[k, s] = lax.dot_general(
-                    half[k * 2 * rows:(k + 1) * 2 * rows], right_v[k, s],
-                    (((1,), (1,)), ((), ())), preferred_element_type=jnp.float32,
-                )
+                terms[k, s] = values[k]
         theirs = pl.multiple_of((1 - core) * rows, rows)
         for g in range(2):
             for t in range(sdev):
                 total = sum(weights[k, s, g, t] * terms[k, s] for k in range(kdev) for s in range(sdev))
                 keep[j, g, t] = total
                 give[j, g, t] = total.astype(jnp.bfloat16)
-        for g in range(2):
             core_copies[j, g] = go(remote(
                 give.at[j, g, :, pl.ds(theirs, rows), :], from_core.at[j, g],
                 core_send.at[j, g], core_recv.at[j, g], {"op": partner},
             ))
 
-    group_of, slots_of = (0, 1, 1), (1, 1, 0)
+    group_of, slots_of, via_neighbour = (0, 1, 1), (1, 1, 0), (1,)
 
     def pair_sum(j, g, r_slot, r=None):
         start, count = (0, rows) if r is None else (r * half_r, half_r)
@@ -181,22 +175,22 @@
         early[j] = pair_sum(j, 0, 0).astype(jnp.bfloat16)
         ahead[j] = go(remote(early.at[j], arrived.at[j], ahead_send.at[j], ahead_recv.at[j], {"sec": after}))
 
-    def is_relay(j):
-        return relayed and j == 3
-
-    def needs_relay(j, r):
-        return relayed and (j, r) in ((1, 1), (2, 0))
+    def is_relay(j, p):
+        return relayed and p in via_neighbour and j == 3
+
+    def needs_relay(j, p, r):
+        return relayed and p in via_neighbour and (j, r) in ((1, 1), (2, 0))
 
     def send_piece(j, p, r):
         value = pair_sum(j, group_of[p], slots_of[p], r)
         rs = slice(r * half_r, (r + 1) * half_r)
         if p == 2:
             value = value + arrived[j, :, rs, :].astype(jnp.float32)
-        if needs_relay(j, r):
+        if needs_relay(j, p, r):
             chip_copies[3, p, r].wait_recv()
             value = value + from_chip[3, p, :, rs, :].astype(jnp.float32)
         sums[j, p, :, rs, :] = value.astype(jnp.bfloat16)
-        via = (1 if r == 0 else 2) if is_relay(j) else j
+        via = (1 if r == 0 else 2) if is_relay(j, p) else j
         chip_copies[j, p, r] = go(remote(
             sums.at[j, p, :, rs, :], from_chip.at[j, p, :, rs, :],
             chip_send.at[j, p, r], chip_recv.at[j, p, r], {"op": peer_of(via)},
@@ -204,46 +198,48 @@
 
     def send_now(j, p):
         for r in (0, 1):
-            if not needs_relay(j, r):
+            if not needs_relay(j, p, r):
                 send_piece(j, p, r)
 
-    def handle(j):
-        send_ahead(j)
-        send_now(j, 0)
+    def relays(p):
+        if relayed and p in via_neighbour:
+            send_piece(1, p, 1)
+            send_piece(2, p, 0)
+
+    def own_now(j):
         core_copies[j, 1].wait_recv()
         send_now(j, 1)
 
-    chunks = list(reversed(order)) + [0]
     for i, j in enumerate(chunks):
         compute(j)
         if i >= 1:
-            handle(chunks[i - 1])
+            send_ahead(chunks[i - 1])
+            send_now(chunks[i - 1], 0)
+        if i >= 2:
+            own_now(chunks[i - 2])
     if order:
-        ahead[order[-1]].wait_recv()
-        send_now(order[-1], 2)
-    if relayed:
-        for p in (0, 1):
-            send_piece(1, p, 1)
-            send_piece(2, p, 0)
+        own_now(chunks[-2])
+        ahead[chunks[0]].wait_recv()
+        send_now(chunks[0], 2)
     send_ahead(0)
     core_copies[0, 1].wait_recv()
-    for j in reversed(order[:-1]):
-        ahead[j].wait_recv()
-        send_now(j, 2)
-    if relayed:
-        send_piece(1, 2, 1)
-        send_piece(2, 2, 0)
-
-    sources = order[:2] if relayed else order
+    relays(1)
+
+    def sources(p):
+        return order[:2] if relayed and p in via_neighbour else order
 
     def collect(p):
         total = pair_sum(0, group_of[p], slots_of[p])
-        for j in sources:
+        for j in sources(p):
             for r in (0, 1):
                 chip_copies[j, p, r].wait_recv()
             total = total + from_chip[j, p].astype(jnp.float32)
         return total
 
+    for j in chunks[1:-1]:
+        ahead[j].wait_recv()
+        send_now(j, 2)
+    relays(2)
     onward[...] = collect(0).astype(jnp.bfloat16)
     shift = go(remote(onward, behind, z_send.at[0], z_recv.at[0], {"sec": after}))
 
@@ -284,6 +280,7 @@
             pltpu.VMEM(right_ops.shape, bf16),
             pltpu.VMEM((n_op, sdev, rows, width), bf16),
             pltpu.VMEM((sdev, width, width), bf16),
+            pltpu.VMEM((chips, kdev, half, 2 * rows, width), f32),
             pltpu.VMEM((chips, 2, sdev, 2 * rows, width), f32),
             pltpu.VMEM((chips, 2, sdev, 2 * rows, width), bf16),
             pltpu.VMEM((chips, 2, sdev, rows, width), bf16),

time: 31.6 us -> 31.1 us (0.984)
  Pallas kernels: 29.9 us -> 29.4 us
    pallas_call x1, Pallas kernels: 29.9 us -> 29.4 us  [on_device(): pl.pallas_call(functools.partial(kernel, n_op, n_sec), out_shape=jax.Shap...]
where the time goes in v3:
time: 31.1 us; the launch traced here: 31 us
  Pallas kernels  29.4 us (95%)
  local copies, waits for them, and re-layouts  1.57 us (5%)
    pallas_call x1, Pallas kernels, on_device(): pl.pallas_call(functools.partial(kernel, n_op, n_sec), out_shape=jax.Shap...  29.4 us
    unnamed x1, local copies, waits for them, and re-layouts  1.57 us

profile of v3, /device:TPU:0, one launch (start us, length us, event | category | flops | bytes accessed | tf_op | source)
XLA Modules:
  0.0 31.0 jit_solution(8609584118028541016)
XLA Ops:
  0.0 29.4 %shard_map.55 = bf16[2,64,512]{2,1,0:T(8,128)(2,1)} custom-call(s32[2,2]{1,0:T(2,128)} %conn_hbm.1, s32[2]{0:T(128)} %dims_hbm.1, bf16[2,64,512]{2,1,0:T(8,128)(2,1)} %psi_ref.1, bf16[2,2,512,512]{3,2,1,0:T(8,128)(2,1)} %left_ref.1, bf16[2,2,512,512]{3,2,1,0:T(8,128)(2,1)} %right_ref.1), custom_call_target="tpu_custom_call" | custom-call | tf_op jit(solution)/shard_map/pallas_call | solution.py:271
  29.4 1.6 %copy.7 = bf16[2,64,512]{2,1,0:T(8,128)(2,1)} copy(bf16[2,64,512]{2,1,0:T(8,128)(2,1)} %shard_map.55) | data formatting | bytes 262144

commit v4 on v3

--- a/solution.py
+++ b/solution.py
@@ -120,7 +120,7 @@
     gather(0)
     load_l.wait()
     load_r.wait()
-    for j in chunks[:2]:
+    for j in chunks[:1]:
         for s in range(half_s):
             for k, value in enumerate(terms_of(j, s)):
                 begun[j, k, s] = value
@@ -141,7 +141,7 @@
     def compute(j):
         terms = {}
         for s in range(sdev):
-            if s < half_s and j in chunks[:2]:
+            if s < half_s and j in chunks[:1]:
                 values = [begun[j, k, s] for k in range(kdev)]
             else:
                 values = terms_of(j, s)

time: 31.1 us -> 30.9 us (level)
  no operation moved by 1% of the time
where the time goes in v4:
time: 30.9 us; the launch traced here: 30.8 us
  Pallas kernels  29.2 us (94%)
  local copies, waits for them, and re-layouts  1.57 us (5%)
    pallas_call x1, Pallas kernels, on_device(): pl.pallas_call(functools.partial(kernel, n_op, n_sec), out_shape=jax.Shap...  29.2 us
    unnamed x1, local copies, waits for them, and re-layouts  1.57 us

profile of v4, /device:TPU:0, one launch (start us, length us, event | category | flops | bytes accessed | tf_op | source)
XLA Modules:
  0.0 30.8 jit_solution(1740584739449881112)
XLA Ops:
  0.0 29.2 %shard_map.55 = bf16[2,64,512]{2,1,0:T(8,128)(2,1)} custom-call(s32[2,2]{1,0:T(2,128)} %conn_hbm.1, s32[2]{0:T(128)} %dims_hbm.1, bf16[2,64,512]{2,1,0:T(8,128)(2,1)} %psi_ref.1, bf16[2,2,512,512]{3,2,1,0:T(8,128)(2,1)} %left_ref.1, bf16[2,2,512,512]{3,2,1,0:T(8,128)(2,1)} %right_ref.1), custom_call_target="tpu_custom_call" | custom-call | tf_op jit(solution)/shard_map/pallas_call | solution.py:271
  29.2 1.6 %copy.7 = bf16[2,64,512]{2,1,0:T(8,128)(2,1)} copy(bf16[2,64,512]{2,1,0:T(8,128)(2,1)} %shard_map.55) | data formatting | bytes 262144
